TPU v7x, 256 devices: a whole 4x4x8 slice. The times are simulated.
256 devices in a mesh: pole: 4 (over y), row: 8 (over z_lo, x), col: 8 (over z_hi, core).
Axes of the slice: x: 4, y: 4, z: 8 (z_hi: 4, z_lo: 2; z = z_hi * 2 + z_lo), core: 2. Of those that a mesh axis runs over, the one named last changes fastest.
Arguments:
- found_inverse: bfloat16 [4, 2, 8192, 8, 8, 128], P('pole', None, 'row', None, 'col'), may hold values from -0.125 to 0.125
- l_panel: bfloat16 [4, 2, 8192, 512], P('pole', None, ('row', 'col')), may hold values from -1.5 to 1.5
- block_pattern: int32 [64, 4], P(('row', 'col')), may hold values 0 or 1
- sup_widths: int32 [4], replicated, may hold values from 1 to 128, 320 in all
- diag_inverse: bfloat16 [4, 2, 512, 128], P('pole'), may hold values from -6 to 6
- pole_weights: float32 [4, 2], P('pole'), may hold values from -4 to 4
Outputs:
- density: float32 [512, 8192], P('col', 'row')
- diagonal: float32 [512, 128], replicated
Inputs may be any that keep to these rules, and one draw needn't show every extreme that they name: `sup_widths`: one supernode has exactly 128 columns.
All inputs are finite; a program needn't handle non-finite values. No bound on the sum of `block_pattern` on one device may be relied on, other than what follows from the above.
Results may differ from a plain program's by a relative error of at most 0.0003.
Values may be sent and summed in bfloat16 or wider, within the bound.
A program may use at most 128 MiB of HBM per device.

v0:
```python
import jax
import jax.numpy as jnp
from jax import lax
from jax.sharding import PartitionSpec as P


def contract(left, right):
    return jnp.einsum("jk,ij->ki", left, right, preferred_element_type=jnp.float32)


def pair_product(left, right):
    return jnp.einsum("ika,kbi->kab", left, right, precision=lax.Precision.HIGHEST)


def per_device(found_inverse, l_panel, block_pattern, sup_widths, diag_inverse, pole_weights):
    slot_width = diag_inverse.shape[-1]
    total_cols = l_panel.shape[-1]
    supernodes = total_cols // slot_width
    row_count = lax.axis_size("row")
    row_index = lax.axis_index("row")
    col_index = lax.axis_index("col")
    columns = jnp.arange(total_cols, dtype=jnp.int32)
    column_ok = columns % slot_width < jnp.repeat(sup_widths, slot_width)
    block_ok = jnp.repeat(block_pattern[0], slot_width) == 1
    masked = jnp.where(
        (column_ok & block_ok)[None, None, :], l_panel[0], jnp.zeros((), jnp.bfloat16)
    )
    column_rows = lax.all_gather(masked, "row", axis=1, tiled=True)
    own_rows = lax.all_gather(masked, "col", axis=1, tiled=True)
    local_rows = found_inverse.shape[2]
    inverse = found_inverse[0].reshape(2, local_rows, row_count * slot_width)
    part_real = contract(column_rows[1], inverse[1]) - contract(column_rows[0], inverse[0])
    part_imag = -(contract(column_rows[1], inverse[0]) + contract(column_rows[0], inverse[1]))
    w_real = pole_weights[0, 0]
    w_imag = pole_weights[0, 1]
    weighted = w_real * part_real - w_imag * part_imag
    part = lax.psum_scatter(weighted, "col", scatter_dimension=0, tiled=True)
    density = lax.psum(part, "pole")
    lifted = own_rows.astype(jnp.float32).reshape(2, local_rows, supernodes, slot_width)
    upper_real = part_real.reshape(supernodes, slot_width, local_rows)
    upper_imag = part_imag.reshape(supernodes, slot_width, local_rows)
    t_real = pair_product(lifted[0], upper_real) - pair_product(lifted[1], upper_imag)
    t_imag = pair_product(lifted[0], upper_imag) + pair_product(lifted[1], upper_real)
    lead_flag = ((row_index == 0) & (col_index == 0)).astype(jnp.float32)
    d_real = diag_inverse[0, 0].astype(jnp.float32).reshape(supernodes, slot_width, slot_width)
    d_imag = diag_inverse[0, 1].astype(jnp.float32).reshape(supernodes, slot_width, slot_width)
    local_term = lead_flag * (w_real * d_real - w_imag * d_imag) - (
        w_real * t_real - w_imag * t_imag
    )
    diagonal = lax.psum(local_term.reshape(total_cols, slot_width), ("pole", "row", "col"))
    return (density, diagonal)


def solution(mesh):
    in_specs = (
        P("pole", None, "row", None, "col", None),
        P("pole", None, ("row", "col"), None),
        P(("row", "col"), None),
        P(),
        P("pole", None, None, None),
        P("pole", None),
    )
    out_specs = (P("col", "row"), P())
    return jax.shard_map(
        per_device, mesh=mesh, in_specs=in_specs, out_specs=out_specs, check_vma=False
    )
```

profile of v0, /device:TPU:2, one launch (start us, length us, event | category | flops | bytes accessed | tf_op | source)
XLA Modules:
  0.0 457.6 jit_solution(11535285280863356408)
XLA Ops:
  7.2 0.0 all-gather.3.cloned.1.call-start
  7.2 0.7 compare_bitcast_fusion
  7.9 0.7 fusion.25
  8.6 1.7 bitcast_select_fusion
  10.3 0.0 all-gather.5.cloned.1.call-start
  10.3 0.7 all-gather.5.cloned.1.call-update
  11.1 0.0 reduce-scatter.2.cloned.1.call-start
  11.1 1.4 fusion.28
  12.5 3.8 fusion.26
  16.3 38.6 %all-gather.3.cloned.1.call-done = bf16[2,1024,512]{2,1,0:T(8,128)(2,1)} async-done(((bf16[2,128,512]{2,1,0:T(8,128)(2,1)}), bf16[2,1024,512]{2,1,0:T(8,128)(2,1)}) %all-gather.3.cloned.1.call-update) | async-done | bytes 2097168 | tf_op jit(solution)/shard_map/all_gather | solution.py:28
  54.9 2.7 fusion.2
  57.6 1.3 fusion
  58.9 0.3 copy-done.2
  59.2 1.3 fusion.12
  60.5 4.6 %multiply_subtract_fusion = (f32[512,1024]{1,0:T(8,128)}, f32[512,1024]{1,0:T(8,128)}) fusion(f32[512,1024]{1,0:T(8,128)S(1)} %fusion.12, f32[]{:T(128)} %bitcast.7, f32[]{:T(128)} %bitcast, f32[512,1024]{1,0:T(8,128)S(1)} %fusion, bf16[128,8,8,128]{3,2,1,0:T(8,128)(2,1)S(1)} %bitcast.67, bf16[2,1024,512]{2,1,0:T(8,128)(2,1)S(1)} %copy-done.3), kind=kOutput, calls=%fused_computation.8 | convolution fusion | flops 1076363264 | bytes 11534344 | tf_op jit(solution)/shard_map/jk,ij->ki/dot_general | solution.py:8
  65.1 0.0 all-reduce.5.cloned.1.call-start
  65.2 0.9 copy-done.4
  66.1 1.3 subtract_multiply_fusion
  67.4 27.9 %all-gather.5.cloned.1.call-done = bf16[2,1024,512]{2,1,0:T(8,128)(2,1)} async-done(((bf16[2,128,512]{2,1,0:T(8,128)(2,1)}), bf16[2,1024,512]{2,1,0:T(8,128)(2,1)}) %all-gather.5.cloned.1.call-update) | async-done | bytes 2097168 | tf_op jit(solution)/shard_map/all_gather | solution.py:29
  95.3 2.7 fusion.27
  97.9 1.3 copy.8
  99.3 1.5 copy.9
  100.8 2.5 fusion.29
  103.3 1.2 fusion.30
  104.5 1.9 fusion.20
  106.4 2.5 fusion.19
  108.9 0.0 all-reduce.3.cloned.1.call-start
  109.0 31.0 %reduce-scatter.2.cloned.1.call-done = f32[64,1024]{1,0:T(8,128)} async-done(((f32[512,1024]{1,0:T(8,128)}), f32[64,1024]{1,0:T(8,128)}) %reduce-scatter.2.cloned.1.call-update) | async-done | bytes 262160 | tf_op jit(solution)/shard_map/reduce_scatter | solution.py:37
  140.1 259.7 %all-reduce.5.cloned.1.call-done = f32[512,128]{1,0:T(8,128)} async-done(((f32[512,128]{1,0:T(8,128)}), f32[512,128]{1,0:T(8,128)}) %all-reduce.5.cloned.1.call-update) | async-done | bytes 262160 | tf_op jit(solution)/shard_map/psum | solution.py:50
  399.8 48.0 %all-reduce.3.cloned.1.call-done = f32[64,1024]{1,0:T(8,128)} async-done(((f32[64,1024]{1,0:T(8,128)}), f32[64,1024]{1,0:T(8,128)}) %all-reduce.3.cloned.1.call-update) | async-done | bytes 262160 | tf_op jit(solution)/shard_map/psum | solution.py:38
  447.8 1.7 copy.36
  449.4 1.7 copy.37
  (12 shorter events, 0.1 us)
Async XLA Ops:
  7.2 47.7 %all-gather.3.cloned.1.call-start = ((), (), s32[]{:S(2)}) async-start(), calls=%async_computation.1 | async-start | bytes 2359296 | tf_op jit(solution)/shard_map/all_gather | solution.py:28
  10.3 85.0 %all-gather.5.cloned.1.call-start = ((), (), s32[]{:S(2)}) async-start(), calls=%async_computation.4 | async-start | bytes 2359296 | tf_op jit(solution)/shard_map/all_gather | solution.py:29
  11.1 129.0 %reduce-scatter.2.cloned.1.call-start = ((), (), s32[]{:S(2)}) async-start(), calls=%async_computation.2 | async-start | bytes 2359296 | tf_op jit(solution)/shard_map/reduce_scatter | solution.py:37
  54.9 2.7 copy-start.3
  57.6 1.6 copy-start.2
  65.1 0.9 copy-start.4
  65.1 334.7 %all-reduce.5.cloned.1.call-start = ((), (), s32[]{:S(2)}) async-start(), calls=%async_computation.5 | async-start | bytes 524288 | tf_op jit(solution)/shard_map/psum | solution.py:50
  100.8 2.6 copy-start
  100.8 2.6 copy-start.1
  108.9 338.8 %all-reduce.3.cloned.1.call-start = ((), (), s32[]{:S(2)}) async-start(), calls=%async_computation.3 | async-start | bytes 524288 | tf_op jit(solution)/shard_map/psum | solution.py:38
Sparse Core Ops, SparseCore 0:
  10.4 44.4 all-gather.2
  57.3 37.9 all-gather.4
  97.8 42.1 reduce-scatter.1
  145.9 253.8 all-reduce.4
  402.0 45.7 all-reduce.2
where the time goes:
time: 458 us
  waiting for transfers between devices  406 us (89%)
  matrix products  18 us (4%)
  local copies, waits for them, and re-layouts  15.2 us (3%)
  between operations  13.9 us (3%)
    psum x1, waiting for transfers between devices, per_device(): lax.psum(local_term.reshape(total_cols, slot_width), ('pole', 'row', 'col'))  260 us
    psum x1, waiting for transfers between devices, per_device(): density = lax.psum(part, 'pole')  48 us
    all_gather x1, waiting for transfers between devices, per_device(): column_rows = lax.all_gather(masked, 'row', axis=1, tiled=True)  38.6 us
    reduce_scatter x1, waiting for transfers between devices, per_device(): part = lax.psum_scatter(weighted, 'col', scatter_dimension=0, tiled=True)  31 us
    all_gather x1, waiting for transfers between devices, per_device(): own_rows = lax.all_gather(masked, 'col', axis=1, tiled=True)  27.9 us
    dot_general x4, matrix products, contract(): jnp.einsum('jk,ij->ki', left, right, preferred_element_type=jnp.float32)  9.92 us
  transfers between devices with their start and end apart: 5, of which 5 were waited for; matrix products, arithmetic and copies ran while one was open for 7% of the time, Pallas kernels for 0%

commit v1 on v0

--- a/solution.py
+++ b/solution.py
@@ -1,7 +1,17 @@
+import functools
 import jax
 import jax.numpy as jnp
 from jax import lax
 from jax.sharding import PartitionSpec as P
+
+
+def _register_turns(payload, which_axis, mesh_dim):
+    for nth in (which_axis, mesh_dim):
+        payload = lax.psum(payload, nth)
+    return payload
+
+
+get_stages_all = functools.partial(_register_turns, which_axis=("row", "col"), mesh_dim="pole")
 
 
 def contract(left, right):
@@ -47,7 +57,7 @@
     local_term = lead_flag * (w_real * d_real - w_imag * d_imag) - (
         w_real * t_real - w_imag * t_imag
     )
-    diagonal = lax.psum(local_term.reshape(total_cols, slot_width), ("pole", "row", "col"))
+    diagonal = get_stages_all(local_term.reshape(total_cols, slot_width))
     return (density, diagonal)
 
 

time: 458 us -> 393 us (0.86)
  waiting for transfers between devices: 406 us -> 344 us
    psum x1, waiting for transfers between devices: 260 us -> 177 us  [_register_turns(): payload = lax.psum(payload, nth)]
    reduce_scatter x1, waiting for transfers between devices: 31 us -> 45 us  [per_device(): part = lax.psum_scatter(weighted, 'col', scatter_dimension=0, tiled=True)]
  transfers between devices with their start and end apart: 5 -> 5, of which waited for: 5 -> 5; matrix products, arithmetic and copies ran while one was open for 7% -> 3% of each run, Pallas kernels for 0% -> 0%
where the time goes in v1:
time: 393 us; the launch traced here: 392 us
  waiting for transfers between devices  344 us (88%)
  matrix products  16.6 us (4%)
  between operations  13.9 us (4%)
  local copies, waits for them, and re-layouts  12.3 us (3%)
  other arithmetic  5.35 us (1%)
    psum x1, waiting for transfers between devices, _register_turns(): payload = lax.psum(payload, nth)  177 us
    psum x1, waiting for transfers between devices, per_device(): density = lax.psum(part, 'pole')  50.6 us
    reduce_scatter x1, waiting for transfers between devices, per_device(): part = lax.psum_scatter(weighted, 'col', scatter_dimension=0, tiled=True)  45 us
    all_gather x1, waiting for transfers between devices, per_device(): column_rows = lax.all_gather(masked, 'row', axis=1, tiled=True)  39.4 us
    all_gather x1, waiting for transfers between devices, per_device(): own_rows = lax.all_gather(masked, 'col', axis=1, tiled=True)  30.4 us
    dot_general x4, matrix products, contract(): jnp.einsum('jk,ij->ki', left, right, preferred_element_type=jnp.float32)  9.97 us
  transfers between devices with their start and end apart: 5, of which 5 were waited for; matrix products, arithmetic and copies ran while one was open for 3% of the time, Pallas kernels for 0%

profile of v1, /device:TPU:2, one launch (start us, length us, event | category | flops | bytes accessed | tf_op | source)
XLA Modules:
  0.0 392.4 jit_solution(14994705129801200079)
XLA Ops:
  7.2 0.0 all-gather.5.cloned.1.call-start
  7.2 0.7 compare_bitcast_fusion
  7.9 0.7 fusion.25
  8.6 1.7 bitcast_select_fusion
  10.3 0.0 all-gather.3.cloned.1.call-start
  10.3 0.7 all-gather.3.cloned.1.call-update
  11.1 0.0 all-reduce.4.cloned.1.call-start
  11.1 1.3 fusion.28
  12.4 2.3 subtract_multiply_fusion
  14.7 4.5 %fusion.26 = (bf16[1,1,1024,8,1,128]{5,3,4,2,1,0:T(8,128)(2,1)}, bf16[1,1,1024,8,1,128]{5,3,4,2,1,0:T(8,128)(2,1)}) fusion(bf16[1,2,1024,8,1,128]{5,3,4,2,1,0:T(8,128)(2,1)} %param.6), kind=kLoop, calls=%fused_computation.33 | loop fusion | bytes 8388608 | tf_op jit(solution)/shard_map/slice | solution.py:42
  19.2 30.4 %all-gather.5.cloned.1.call-done = bf16[2,1024,512]{2,1,0:T(8,128)(2,1)} async-done(((bf16[2,128,512]{2,1,0:T(8,128)(2,1)}), bf16[2,1024,512]{2,1,0:T(8,128)(2,1)}) %all-gather.5.cloned.1.call-update) | async-done | bytes 2097168 | tf_op jit(solution)/shard_map/all_gather | solution.py:39
  49.6 1.7 fusion.27
  51.3 0.5 copy.8
  51.9 0.5 copy.9
  52.4 39.4 %all-gather.3.cloned.1.call-done = bf16[2,1024,512]{2,1,0:T(8,128)(2,1)} async-done(((bf16[2,128,512]{2,1,0:T(8,128)(2,1)}), bf16[2,1024,512]{2,1,0:T(8,128)(2,1)}) %all-gather.3.cloned.1.call-update) | async-done | bytes 2097168 | tf_op jit(solution)/shard_map/all_gather | solution.py:38
  91.8 3.4 fusion.2
  95.2 1.3 fusion.12
  96.5 1.2 fusion.29
  97.7 0.4 copy-done.1
  98.1 1.3 fusion
  99.4 4.0 %multiply_subtract_fusion = (f32[512,1024]{1,0:T(8,128)}, f32[512,1024]{1,0:T(8,128)S(1)}) fusion(f32[512,1024]{1,0:T(8,128)S(1)} %fusion.12, f32[]{:T(128)} %bitcast.7, f32[]{:T(128)} %bitcast, f32[512,1024]{1,0:T(8,128)S(1)} %fusion, bf16[128,8,8,128]{3,2,1,0:T(8,128)(2,1)S(1)} %bitcast.67, bf16[2,1024,512]{2,1,0:T(8,128)(2,1)S(1)} %copy-done.2), kind=kOutput, calls=%fused_computation.8 | convolution fusion | flops 1076363264 | bytes 11534344 | tf_op jit(solution)/shard_map/jk,ij->ki/dot_general | solution.py:18
  103.4 1.2 fusion.30
  104.6 1.8 fusion.20
  106.4 2.5 fusion.19
  108.9 0.0 reduce-scatter.2.cloned.1.call-start
  109.0 0.5 reduce-scatter.2.cloned.1.call-update
  109.5 0.0 all-reduce.6.cloned.1.call-start
  109.6 177.4 %all-reduce.4.cloned.1.call-done = f32[512,128]{1,0:T(8,128)} async-done(((f32[512,128]{1,0:T(8,128)}), f32[512,128]{1,0:T(8,128)}) %all-reduce.4.cloned.1.call-update) | async-done | bytes 262160 | tf_op jit(solution)/shard_map/psum | solution.py:10
  287.0 45.0 %reduce-scatter.2.cloned.1.call-done = f32[64,1024]{1,0:T(8,128)} async-done(((f32[512,1024]{1,0:T(8,128)}), f32[64,1024]{1,0:T(8,128)}) %reduce-scatter.2.cloned.1.call-update) | async-done | bytes 262160 | tf_op jit(solution)/shard_map/reduce_scatter | solution.py:47
  332.0 50.6 %all-reduce.6.cloned.1.call-done = (f32[64,1024]{1,0:T(8,128)}, f32[512,128]{1,0:T(8,128)}) async-done(((f32[64,1024]{1,0:T(8,128)}, f32[512,128]{1,0:T(8,128)}), (f32[64,1024]{1,0:T(8,128)}, f32[512,128]{1,0:T(8,128)})) %all-reduce.6.cloned.1.call-update) | async-done | bytes 524304 | tf_op jit(solution)/shard_map/psum | solution.py:48
  382.6 1.7 copy.37
  384.2 1.7 copy.38
  (8 shorter events, 0.1 us)
Async XLA Ops:
  7.2 42.5 %all-gather.5.cloned.1.call-start = ((), (), s32[]{:S(2)}) async-start(), calls=%async_computation.3 | async-start | bytes 2359296 | tf_op jit(solution)/shard_map/all_gather | solution.py:39
  10.3 81.5 %all-gather.3.cloned.1.call-start = ((), (), s32[]{:S(2)}) async-start(), calls=%async_computation.1 | async-start | bytes 2359296 | tf_op jit(solution)/shard_map/all_gather | solution.py:38
  11.1 275.9 %all-reduce.4.cloned.1.call-start = ((), (), s32[]{:S(2)}) async-start(), calls=%async_computation.4 | async-start | bytes 524288 | tf_op jit(solution)/shard_map/psum | solution.py:10
  91.8 3.4 copy-start
  91.8 3.4 copy-start.2
  96.5 1.6 copy-start.1
  108.9 223.0 %reduce-scatter.2.cloned.1.call-start = ((), (), s32[]{:S(2)}) async-start(), calls=%async_computation.2 | async-start | bytes 2359296 | tf_op jit(solution)/shard_map/reduce_scatter | solution.py:47
  109.5 273.0 %all-reduce.6.cloned.1.call-start = ((), (), s32[]{:S(2)}) async-start(), calls=%async_computation.5 | async-start | bytes 1048576 | tf_op jit(solution)/shard_map/psum | solution.py:48
Sparse Core Ops, SparseCore 0:
  10.4 39.1 all-gather.4
  52.0 39.7 all-gather.2
  109.1 177.8 all-reduce.3
  289.4 42.5 reduce-scatter.1
  334.2 48.2 all-reduce.5
